TPU v7x, 256 devices: a whole 4x4x8 slice. The times are simulated.
256 devices in a mesh: dp: 8 (over x, core), seq: 32 (over z, y).
Axes of the slice: x: 4, y: 4, z: 8, core: 2. Of those that a mesh axis runs over, the one named last changes fastest.
Arguments:
- queries: bfloat16 [8, 8192, 2048], P('dp', 'seq'), may hold values from -40 to 40
- keys: bfloat16 [8, 8192, 2048], P('dp', 'seq'), may hold values from -40 to 40
- values: bfloat16 [8, 8192, 2048], P('dp', 'seq'), may hold values from -6 to 6
- key_gain: float32 [2048], replicated, may hold values from 0.25 to 1.75
- random_blocks: int32 [16, 128, 3], P(None, 'seq'), may hold values from 2 to 127, as said below
- out_grad: bfloat16 [8, 8192, 2048], P('dp', 'seq'), may hold values from -6 to 6
Outputs:
- attended: bfloat16 [8, 8192, 2048], P('dp', 'seq')
- query_grad: bfloat16 [8, 8192, 2048], P('dp', 'seq')
- key_grad: bfloat16 [8, 8192, 2048], P('dp', 'seq')
- value_grad: bfloat16 [8, 8192, 2048], P('dp', 'seq')
- gain_grad: float32 [2048], replicated
Inputs may be any that keep to these rules, and one draw needn't show every extreme that they name: `random_blocks`: for the 4 query blocks of one device, all heads and entries together, at most 9 entries name blocks held by any one device (blocks d * 4 to d * 4 + 3), and exactly 9 name the blocks of some device.
All inputs are finite; a program needn't handle non-finite values.
Results may differ from a plain program's by a relative error of at most 0.03.
The roundings to bfloat16 on the way count: a program that leaves them out, or rounds other values in their place, can miss the bound.
Values may be sent and summed in bfloat16 or wider, within the bound.
No kernel may reach another device: no remote copies, remote signals or barrier semaphores. Data moves between devices by JAX's collectives and lax.ppermute only.
A program may use at most 128 MiB of HBM per device.

v0:
```python
import math
import jax
import jax.numpy as jnp
from jax import lax
from jax.sharding import PartitionSpec as P

HEADS = 16
HD = 128
BLOCK = 64
NG = 2
NR = 3
NK = 8
NEGATIVE = -1e30


def broadcast(block, axis, owner):
    block = jnp.where(lax.axis_index(axis) == owner, block, jnp.zeros_like(block))
    return lax.psum(block, axis)


def padded_2(cells, sides, width):
    for axis, dim in sides:
        count = lax.axis_size(axis)
        ends = count - 1
        head = lax.slice_in_dim(cells, 0, width, axis=dim)
        tail = lax.slice_in_dim(cells, cells.shape[dim] - width, cells.shape[dim], axis=dim)
        cells = jnp.concatenate(
            [
                lax.ppermute(tail, axis, [(i, (i + 1) % count) for i in range(ends)]),
                cells,
                lax.ppermute(head, axis, [((i + 1) % count, i) for i in range(ends)]),
            ],
            axis=dim,
        )
    return cells


def passed_along(array, axis, by):
    length = lax.axis_size(axis)
    pairs = [(i, i + by) for i in range(length) if 0 <= i + by < length]
    return lax.ppermute(array, axis, pairs)


def to_heads(rows_in):
    return rows_in.reshape(rows_in.shape[0] // BLOCK, BLOCK, HEADS, HD).transpose(2, 0, 1, 3)


def from_heads(blocks_in):
    return blocks_in.transpose(1, 2, 0, 3).reshape(1, blocks_in.shape[1] * BLOCK, HEADS * HD)


def build_list(edge_part, window_part, random_in):
    head_count = random_in.shape[0]
    block_count = random_in.shape[1]
    global_list = jnp.broadcast_to(
        edge_part[:, None], (head_count, block_count) + edge_part.shape[1:]
    )
    window_list = jnp.stack(
        [window_part[:, offset : offset + block_count] for offset in range(3)], axis=2
    )
    joined = jnp.concatenate([global_list, window_list, random_in], axis=2)
    return joined.reshape(head_count, block_count, NK * BLOCK, HD)


def spread_terms(coef, rows_in):
    head_count = rows_in.shape[0]
    block_count = rows_in.shape[1]
    coef_blocks = coef.reshape(head_count, block_count, BLOCK, NK, BLOCK)
    global_term = jnp.einsum(
        "hpbgc,hpbd->hgcd", coef_blocks[:, :, :, :NG], rows_in, preferred_element_type=jnp.float32
    )
    padded = jnp.zeros((head_count, block_count + 2, BLOCK, HD), jnp.float32)
    for offset in range(3):
        term = jnp.einsum(
            "hpbc,hpbd->hpcd",
            coef_blocks[:, :, :, NG + offset],
            rows_in,
            preferred_element_type=jnp.float32,
        )
        padded = padded + jnp.pad(term, ((0, 0), (offset, 2 - offset), (0, 0), (0, 0)))
    random_term = jnp.einsum(
        "hpbrc,hpbd->hprcd",
        coef_blocks[:, :, :, NG + 3 :],
        rows_in,
        preferred_element_type=jnp.float32,
    )
    return (global_term, padded, random_term)


def sparse_group(
    query_blk,
    edge_key,
    edge_value,
    window_key,
    window_value,
    random_key,
    random_value,
    grad_blk,
    valid_keys,
    keep_rows,
):
    score_scale = HD ** (-0.5)
    key_list = build_list(edge_key, window_key, random_key)
    value_list = build_list(edge_value, window_value, random_value)
    key_mask = jnp.repeat(valid_keys, BLOCK, axis=1)[None, :, None, :]
    scores = (
        jnp.einsum("hpbd,hpnd->hpbn", query_blk, key_list, preferred_element_type=jnp.float32)
        * score_scale
    )
    scores = jnp.where(key_mask, scores, NEGATIVE)
    row_top = jnp.max(scores, axis=3, keepdims=True)
    expo_vals = jnp.where(key_mask, jnp.exp(scores - row_top), 0.0)
    row_total = jnp.sum(expo_vals, axis=3, keepdims=True)
    numerator = jnp.einsum(
        "hpbn,hpnd->hpbd",
        expo_vals.astype(jnp.bfloat16),
        value_list,
        preferred_element_type=jnp.float32,
    )
    attended = (numerator / row_total).astype(jnp.bfloat16)
    row_delta = jnp.sum(grad_blk.astype(jnp.float32) * attended.astype(jnp.float32), axis=3)
    weights = expo_vals / row_total * keep_rows[None, :, None, None]
    dprobs = jnp.einsum("hpbd,hpnd->hpbn", grad_blk, value_list, preferred_element_type=jnp.float32)
    dscores = (weights * (dprobs - row_delta[:, :, :, None]) * score_scale).astype(jnp.bfloat16)
    dquery = jnp.einsum("hpbn,hpnd->hpbd", dscores, key_list, preferred_element_type=jnp.float32)
    key_global, key_padded, key_random = spread_terms(dscores, query_blk)
    value_global, value_padded, value_random = spread_terms(weights.astype(jnp.bfloat16), grad_blk)
    global_part = jnp.stack([key_global, value_global], axis=1)
    padded = jnp.stack([key_padded, value_padded], axis=1)
    random_part = jnp.stack([key_random, value_random], axis=1)
    return (attended, dquery, global_part, padded, random_part)


def shards(queries, keys, values, key_gain, random_blocks, out_grad):
    score_scale = HD ** (-0.5)
    tok_count = queries.shape[1]
    per_dev = tok_count // BLOCK
    owners = lax.axis_size("seq")
    seq_place = lax.axis_index("seq")
    total_blocks = owners * per_dev
    first_block = seq_place * per_dev
    key_eff = (keys[0].astype(jnp.float32) * key_gain).astype(jnp.bfloat16)
    edge_count = NG * BLOCK
    edge_rows = broadcast(
        jnp.stack(
            [
                queries[0, :edge_count],
                key_eff[:edge_count],
                values[0, :edge_count],
                out_grad[0, :edge_count],
            ]
        ),
        "seq",
        0,
    )
    window_rows = padded_2(jnp.stack([key_eff, values[0]]), (("seq", 1),), BLOCK)
    query_h = to_heads(queries[0])
    key_h = to_heads(key_eff)
    value_h = to_heads(values[0])
    grad_h = to_heads(out_grad[0])
    edge_heads = [to_heads(edge_rows[slot_pick]) for slot_pick in range(4)]
    window_key = to_heads(window_rows[0])
    window_value = to_heads(window_rows[1])
    request_count = HEADS * per_dev * NR
    capacity = (request_count + owners - 1) // owners + 3
    target = random_blocks.reshape(request_count)
    owner_dev = target // per_dev
    table_index = (
        jnp.arange(request_count, dtype=jnp.int32) // (per_dev * NR) * per_dev + target % per_dev
    )
    onehot = (owner_dev[:, None] == jnp.arange(owners, dtype=jnp.int32)[None, :]).astype(jnp.int32)
    before = jnp.cumsum(onehot, axis=0) - onehot
    slot_rank = jnp.sum(before * onehot, axis=1)
    position = owner_dev * capacity + slot_rank
    outgoing = (
        jnp.full((owners * capacity,), -1, jnp.int32)
        .at[position]
        .set(table_index)
        .reshape(owners, capacity)
    )
    kv_table = jnp.concatenate([key_h, value_h], axis=3).reshape(HEADS * per_dev, BLOCK, 2 * HD)
    index_part = lax.all_to_all(outgoing, "seq", split_axis=0, concat_axis=0, tiled=True)
    picked = kv_table[jnp.clip(index_part, 0, HEADS * per_dev - 1)]
    fetch_result = (
        lax.all_to_all(picked, "seq", split_axis=0, concat_axis=0, tiled=True),
        index_part,
    )
    arrived, served = fetch_result
    fetched = arrived.reshape(owners * capacity, BLOCK, 2 * HD)[position].reshape(
        HEADS, per_dev, NR, BLOCK, 2 * HD
    )
    fetched_key = fetched[..., :HD]
    fetched_value = fetched[..., HD:]
    block_index = first_block + jnp.arange(per_dev, dtype=jnp.int32)
    window_index = block_index[:, None] + jnp.arange(-1, 2, dtype=jnp.int32)[None, :]
    valid_keys = jnp.concatenate(
        [
            jnp.ones((per_dev, NG), bool),
            (window_index >= NG) & (window_index < total_blocks),
            jnp.ones((per_dev, NR), bool),
        ],
        axis=1,
    )
    keep_rows = (block_index >= NG).astype(jnp.float32)
    group_size = math.gcd(HEADS, 4)

    def by_group(array_in):
        return array_in.reshape((HEADS // group_size, group_size) + array_in.shape[1:])

    def merge_groups(array_in):
        return array_in.reshape((HEADS,) + array_in.shape[2:])

    def run_group(bundle):
        return sparse_group(
            bundle[0],
            bundle[1],
            bundle[2],
            bundle[3],
            bundle[4],
            bundle[5],
            bundle[6],
            bundle[7],
            valid_keys,
            keep_rows,
        )

    grouped = lax.map(
        run_group,
        (
            by_group(query_h),
            by_group(edge_heads[1]),
            by_group(edge_heads[2]),
            by_group(window_key),
            by_group(window_value),
            by_group(fetched_key),
            by_group(fetched_value),
            by_group(grad_h),
        ),
    )
    attended_h, dquery_h, global_part, padded, random_part = [
        merge_groups(piece_out) for piece_out in grouped
    ]
    edge_query = edge_heads[0].reshape(HEADS, edge_count, HD)
    edge_grad = edge_heads[3].reshape(HEADS, edge_count, HD)
    flat_key = key_h.reshape(HEADS, tok_count, HD)
    flat_value = value_h.reshape(HEADS, tok_count, HD)
    edge_scores = (
        jnp.einsum("hqd,htd->hqt", edge_query, flat_key, preferred_element_type=jnp.float32)
        * score_scale
    )
    edge_top = lax.pmax(jnp.max(edge_scores, axis=2), "seq")
    edge_expo = jnp.exp(edge_scores - edge_top[:, :, None])
    edge_total, edge_numer = lax.psum(
        (
            jnp.sum(edge_expo, axis=2),
            jnp.einsum(
                "hqt,htd->hqd",
                edge_expo.astype(jnp.bfloat16),
                flat_value,
                preferred_element_type=jnp.float32,
            ),
        ),
        "seq",
    )
    edge_out = (edge_numer / edge_total[:, :, None]).astype(jnp.bfloat16)
    edge_delta = jnp.sum(edge_grad.astype(jnp.float32) * edge_out.astype(jnp.float32), axis=2)
    edge_weights = edge_expo / edge_total[:, :, None]
    edge_dprobs = jnp.einsum(
        "hqd,htd->hqt", edge_grad, flat_value, preferred_element_type=jnp.float32
    )
    edge_dscores = (edge_weights * (edge_dprobs - edge_delta[:, :, None]) * score_scale).astype(
        jnp.bfloat16
    )
    edge_dquery = jnp.einsum(
        "hqt,htd->hqd", edge_dscores, flat_key, preferred_element_type=jnp.float32
    )
    local_dkey = jnp.einsum(
        "hqt,hqd->htd", edge_dscores, edge_query, preferred_element_type=jnp.float32
    )
    local_dvalue = jnp.einsum(
        "hqt,hqd->htd",
        edge_weights.astype(jnp.bfloat16),
        edge_grad,
        preferred_element_type=jnp.float32,
    )
    random_rounded = (
        random_part.transpose(0, 2, 3, 4, 1, 5)
        .reshape(request_count, BLOCK, 2 * HD)
        .astype(jnp.bfloat16)
    )
    sendback = (
        jnp.zeros((owners * capacity, BLOCK, 2 * HD), jnp.bfloat16)
        .at[position]
        .set(random_rounded)
        .reshape(owners, capacity, BLOCK, 2 * HD)
    )
    returned = lax.all_to_all(sendback, "seq", split_axis=0, concat_axis=0, tiled=True)
    owner_table = (
        served.reshape(1, owners * capacity)
        == jnp.arange(HEADS * per_dev, dtype=jnp.int32)[:, None]
    ).astype(jnp.bfloat16)
    summed = jnp.dot(
        owner_table,
        returned.reshape(owners * capacity, BLOCK * 2 * HD),
        preferred_element_type=jnp.float32,
    )
    summed = summed.reshape(HEADS, per_dev, BLOCK, 2, HD).transpose(0, 3, 1, 2, 4)
    from_right = passed_along(padded[:, :, 0].astype(jnp.bfloat16), "seq", -1).astype(jnp.float32)
    from_left = passed_along(padded[:, :, per_dev + 1].astype(jnp.bfloat16), "seq", 1).astype(
        jnp.float32
    )
    edge_dquery_sum, global_sum = lax.psum((edge_dquery, global_part), "seq")
    accum = padded[:, :, 1 : per_dev + 1]
    accum = accum + jnp.stack([local_dkey, local_dvalue], axis=1).reshape(
        HEADS, 2, per_dev, BLOCK, HD
    )
    accum = accum + summed
    accum = accum.at[:, :, per_dev - 1].add(from_right)
    accum = accum.at[:, :, 0].add(from_left)
    is_first = (seq_place == 0).astype(jnp.float32)
    accum = accum.at[:, :, :NG].add(global_sum * is_first)
    is_edge = (block_index < NG)[None, :, None, None]
    tail_zeros = jnp.zeros((HEADS, per_dev - NG, BLOCK, HD), jnp.float32)
    edge_dq_blocks = jnp.concatenate(
        [edge_dquery_sum.reshape(HEADS, NG, BLOCK, HD), tail_zeros], axis=1
    )
    edge_out_blocks = jnp.concatenate(
        [edge_out.reshape(HEADS, NG, BLOCK, HD), tail_zeros.astype(jnp.bfloat16)], axis=1
    )
    dquery_all = jnp.where(is_edge, edge_dq_blocks, dquery_h).astype(jnp.bfloat16)
    attended_all = jnp.where(is_edge, edge_out_blocks, attended_h)
    key_eff_grad = accum[:, 0]
    gain_heads = key_gain.reshape(HEADS, HD)
    key_grad_h = (key_eff_grad * gain_heads[:, None, None, :]).astype(jnp.bfloat16)
    value_grad_h = accum[:, 1].astype(jnp.bfloat16)
    gain_term = jnp.sum(key_eff_grad * to_heads(keys[0]).astype(jnp.float32), axis=(1, 2)).reshape(
        HEADS * HD
    )
    gain_grad = lax.psum(gain_term, ("dp", "seq"))
    return (
        from_heads(attended_all),
        from_heads(dquery_all),
        from_heads(key_grad_h),
        from_heads(value_grad_h),
        gain_grad,
    )


def solution(mesh):
    placed = (
        P("dp", "seq", None),
        P("dp", "seq", None),
        P("dp", "seq", None),
        P(),
        P(None, "seq", None),
        P("dp", "seq", None),
    )
    return jax.shard_map(
        shards,
        mesh=mesh,
        in_specs=placed,
        out_specs=(
            P("dp", "seq", None),
            P("dp", "seq", None),
            P("dp", "seq", None),
            P("dp", "seq", None),
            P(),
        ),
        check_vma=False,
    )
```

profile of v0, /device:TPU:1, one launch (start us, length us, event | category | flops | bytes accessed | tf_op | source)
XLA Modules:
  0.0 1441.6 jit_solution(389370633972243564)
XLA Ops:
  11.2 12.0 all-to-all-start
  23.2 2.8 convert_bitcast_fusion
  33.7 10.3 gather_fusion
  43.9 7.5 all-to-all-start.1
  58.0 3.9 collective-permute-start
  68.2 25.1 %collective-permute-done = bf16[2,64,2048]{2,1,0:T(8,128)(2,1)} collective-permute-done((bf16[2,64,2048]{2,1,0:T(8,128)(2,1)}, bf16[2,64,2048]{2,1,0:T(8,128)(2,1)}, u32[]{:S(2)}, u32[]{:S(2)}) %collective-permute-start) | collective-permute-done | bytes 524320 | tf_op jit(solution)/shard_map/ppermute | solution.py:29
  93.3 21.3 %collective-permute-done.1 = bf16[2,64,2048]{2,1,0:T(8,128)(2,1)} collective-permute-done((bf16[2,64,2048]{2,1,0:T(8,128)(2,1)}, bf16[2,64,2048]{2,1,0:T(8,128)(2,1)}, u32[]{:S(2)}, u32[]{:S(2)}) %collective-permute-start.1) | collective-permute-done | bytes 524320 | tf_op jit(solution)/shard_map/ppermute | solution.py:31
  119.1 206.0 %all-reduce.14.cloned.1.call-done = bf16[4,128,2048]{2,1,0:T(8,128)(2,1)} async-done(((bf16[4,128,2048]{2,1,0:T(8,128)(2,1)}), bf16[4,128,2048]{2,1,0:T(8,128)(2,1)}) %all-reduce.14.cloned.1.call-update) | async-done | bytes 2097168 | tf_op jit(solution)/shard_map/psum | solution.py:18
  329.1 11.8 gather_fusion.1
  340.9 8.0 fusion.134
  348.9 287.8 %while.24 = (s32[]{:T(128)}, bf16[4,4,4,64,128]{4,3,2,1,0:T(8,128)(2,1)}, bf16[4,4,4,64,128]{4,3,2,1,0:T(8,128)(2,1)}, f32[4,4,2,2,64,128]{5,1,0,2,4,3:T(4,128)}...) while((s32[]{:T(128)}, ...), condition=%wide.region_14.15_spmd.clone, body=%wide.region_10.14_spmd.clone.sunk | while | flops 952370176 | bytes 142396560 | solution.py:227
  356.1 3.5 fusion.232
  365.5 3.1 fusion.233
  368.6 5.1 bitcast_dynamic-update-slice_fusion.6
  374.9 3.2 multiply_convert_fusion.4
  385.4 2.9 fusion.240
  427.9 3.5 fusion.232
  437.3 3.1 fusion.233
  440.4 5.1 bitcast_dynamic-update-slice_fusion.6
  446.7 3.2 multiply_convert_fusion.4
  457.1 2.9 fusion.240
  499.7 3.5 fusion.232
  509.1 3.1 fusion.233
  512.2 5.1 bitcast_dynamic-update-slice_fusion.6
  518.5 3.2 multiply_convert_fusion.4
  529.0 2.9 fusion.240
  571.5 3.5 fusion.232
  580.9 3.1 fusion.233
  584.1 5.1 bitcast_dynamic-update-slice_fusion.6
  590.4 3.2 multiply_convert_fusion.4
  600.7 2.9 fusion.240
  636.7 12.7 copy.168
  649.4 10.8 reshape.529
  660.3 4.9 broadcast_in_dim.167
  665.1 29.1 %scatter_fusion = bf16[288,64,256]{2,1,0:T(8,128)(2,1)} fusion(bf16[288,64,256]{2,1,0:T(8,128)(2,1)} %broadcast_in_dim.167, s32[192]{0:T(256)S(1)} %bitcast.511, bf16[192,64,256]{2,1,0:T(8,128)(2,1)} %reshape.529), kind=kCustom, calls=%fused_computation.3 | custom fusion | bytes 18875136 | tf_op jit(solution)/shard_map/scatter | solution.py:294
  694.3 6.0 all-to-all-start.2
  704.3 248.7 %pmax.7 = f32[16,128]{1,0:T(8,128)S(1)} all-reduce(f32[16,128]{1,0:T(8,128)S(1)} %get-tuple-element.352), channel_id=1, replica_groups=mesh['dp'=8,'seq'=32] {'seq'}, use_global_device_ids=true, to_apply=%region_2.3 | all-reduce | flops 2048 | bytes 16384 | tf_op jit(solution)/shard_map/pmax | solution.py:251
  953.0 3.5 fusion.97
  960.4 59.2 %psum.44 = f32[16,128]{1,0:T(8,128)S(1)} all-reduce(f32[16,128]{1,0:T(8,128)S(1)} %fusion.95), channel_id=1, replica_groups=mesh['dp'=8,'seq'=32] {'seq'}, use_global_device_ids=true, to_apply=%region_5.6 | all-reduce | flops 2048 | bytes 16384 | tf_op jit(solution)/shard_map/psum | solution.py:253
  1019.5 2.9 fusion.104
  1028.2 4.8 collective-permute-start.3
  1033.0 99.2 %all-reduce.16.cloned.1.call-done = (f32[16,128,128]{2,1,0:T(8,128)}, f32[16,2,2,64,128]{4,0,1,3,2:T(8,128)}) async-done(((f32[16,128,128]{2,1,0:T(8,128)}, f32[16,2,2,64,128]{4,0,1,3,2:T(8,128)}), (f32[16,128,128]{2,1,0:T(8,128)}, f32[16,2,2,64,128]{4,0,1,3,2:T(8,128)})) %all-reduce.16.cloned.1.call-update) | async-done | bytes 3145744 | tf_op jit(solution)/shard_map/psum | solution.py:253
  1141.9 123.4 %all-reduce.17 = bf16[16,2,64,128]{3,2,1,0:T(8,128)(2,1)S(1)} all-reduce(f32[16,2,64,128]{3,2,1,0:T(8,128)} %bitcast.485), channel_id=1, replica_groups=mesh['dp'=8,'seq'=32] {'seq'}, use_global_device_ids=true, to_apply=%region_16.17 | all-reduce | flops 262144 | bytes 1572864 | tf_op jit(solution)/shard_map/psum | solution.py:312
  1265.3 2.9 fusion.93
  1273.5 18.5 %copy.212 = bf16[36,8,64,256]{3,1,2,0:T(8,128)(2,1)} copy(bf16[36,8,64,256]{3,2,1,0:T(8,128)(2,1)} %bitcast.182) | data formatting | bytes 18874368
  1292.0 16.1 %dot_general.116 = bf16[64,2,128,288]{2,1,0,3:T(2,128)(2,1)} reshape(bf16[16384,288]{0,1:T(8,128)(2,1)} %bitcast.460) | data formatting | bytes 18874368 | tf_op jit(solution)/shard_map/dot_general | solution.py:302
  1308.1 12.3 fusion.85
  1328.3 106.2 %psum.47 = f32[2048]{0:T(1024)} all-reduce(f32[2048]{0:T(1024)S(1)} %bitcast.508), channel_id=1, replica_groups=mesh['dp'=8,'seq'=32] {'dp','seq'}, use_global_device_ids=true, to_apply=%region_20.21 | all-reduce | flops 2048 | bytes 16384 | tf_op jit(solution)/shard_map/psum | solution.py:339
  (453 shorter events, 283.5 us)
Async XLA Ops:
  9.3 58.8 %copy-start.31 = (s32[192,1]{0,1:T(1,128)}, s32[192,1]{0,1:T(1,128)S(1)}, u32[]{:S(2)}) copy-start(s32[192,1]{0,1:T(1,128)S(1)} %compare_select_fusion.1) | copy-start | bytes 2308
  11.2 20.6 %all-to-all-start = ((s32[32,1,9]{2,1,0:T(1,128)}), s32[32,1,9]{2,1,0:T(1,128)S(1)}, u32[]{:S(2)}, u32[]{:S(2)}) async-start(s32[32,1,9]{2,1,0:T(1,128)} %bitcast.20), calls=%async_computation | async-start | bytes 32768 | tf_op jit(solution)/shard_map/all_to_all | solution.py:182
  26.5 2.3 copy-start.6
  43.9 285.2 %all-to-all-start.1 = ((bf16[32,9,64,256]{3,2,1,0:T(8,128)(2,1)}), bf16[32,9,64,256]{3,2,1,0:T(8,128)(2,1)}, u32[]{:S(2)}, u32[]{:S(2)}) async-start(bf16[32,9,64,256]{3,2,1,0:T(8,128)(2,1)} %bitcast.459), calls=%async_computation.1 | async-start | bytes 18874368 | tf_op jit(solution)/shard_map/all_to_all | solution.py:185
  51.4 273.7 %all-reduce.14.cloned.1.call-start = ((), (), s32[]{:S(2)}) async-start(), calls=%async_computation.3 | async-start | bytes 4194304 | tf_op jit(solution)/shard_map/psum | solution.py:18
  58.0 35.3 %collective-permute-start = (bf16[2,64,2048]{2,1,0:T(8,128)(2,1)}, bf16[2,64,2048]{2,1,0:T(8,128)(2,1)}, u32[]{:S(2)}, u32[]{:S(2)}) collective-permute-start(bf16[2,64,2048]{2,1,0:T(8,128)(2,1)} %get-tuple-element.342), channel_id=1, source_target_pairs={{0,1},{1,2},{2,3},{3,4},{4,5},{5,6},{6,7},{7,8},{8,9},{9,10},{10,1... | collective-permute-start | bytes 1572872 | tf_op jit(solution)/shard_map/ppermute | solution.py:29
  61.8 52.8 %collective-permute-start.1 = (bf16[2,64,2048]{2,1,0:T(8,128)(2,1)}, bf16[2,64,2048]{2,1,0:T(8,128)(2,1)}, u32[]{:S(2)}, u32[]{:S(2)}) collective-permute-start(bf16[2,64,2048]{2,1,0:T(8,128)(2,1)} %get-tuple-element.343), channel_id=1, source_target_pairs={{1,0},{2,1},{3,2},{4,3},{5,4},{6,5},{7,6},{8,7},{9,8},{10,9},{11,1... | collective-permute-start | bytes 1572872 | tf_op jit(solution)/shard_map/ppermute | solution.py:31
  63.7 2.8 copy-start.22
  355.9 3.7 copy-start.1
  362.6 2.9 copy-start.2
  380.2 3.8 copy-start.5
  382.5 2.9 copy-start
  409.9 2.6 copy-start.4
  416.6 2.7 copy-start.3
  416.6 2.7 copy-start.26
  427.7 3.7 copy-start.1
  434.4 2.9 copy-start.2
  452.0 3.8 copy-start.5
  454.3 2.9 copy-start
  481.7 2.6 copy-start.4
  488.4 2.7 copy-start.3
  488.4 2.6 copy-start.26
  499.5 3.7 copy-start.1
  506.2 2.9 copy-start.2
  523.8 3.8 copy-start.5
  526.0 3.0 copy-start
  553.5 2.6 copy-start.4
  560.2 2.7 copy-start.3
  560.3 2.7 copy-start.26
  571.3 3.7 copy-start.1
  578.0 2.9 copy-start.2
  595.6 3.8 copy-start.5
  597.9 2.8 copy-start
  625.3 2.6 copy-start.4
  632.0 2.7 copy-start.3
  632.0 2.7 copy-start.26
  660.3 4.9 copy-start.32
  694.3 6.1 copy-start.7
  694.3 6.1 copy-start.29
  694.3 579.3 %all-to-all-start.2 = ((bf16[32,9,64,256]{3,2,1,0:T(8,128)(2,1)}), bf16[32,9,64,256]{3,2,1,0:T(8,128)(2,1)}, u32[]{:S(2)}, u32[]{:S(2)}) async-start(bf16[32,9,64,256]{3,2,1,0:T(8,128)(2,1)} %bitcast.457), calls=%async_computation.2 | async-start | bytes 18874368 | tf_op jit(solution)/shard_map/all_to_all | solution.py:297
  700.3 432.0 %all-reduce.16.cloned.1.call-start = ((), (), s32[]{:S(2)}) async-start(), calls=%async_computation.4 | async-start | bytes 6291456 | tf_op jit(solution)/shard_map/psum | solution.py:253
  1019.5 5.5 slice-start.1
  1019.5 5.5 slice-start.2
  1026.9 293.5 %collective-permute-start.2 = (bf16[16,2,64,128]{3,0,1,2:T(8,128)(2,1)}, bf16[16,2,64,128]{3,0,1,2:T(8,128)(2,1)}, u32[]{:S(2)}, u32[]{:S(2)}) collective-permute-start(bf16[16,2,64,128]{3,0,1,2:T(8,128)(2,1)} %get-tuple-element.335), channel_id=1, source_target_pairs={{1,0},{2,1},{3,2},{4,3},{5,4},{6,5},{7,6},{8,7},{9,8},{10,9},{11,1... | collective-permute-start | bytes 1572872 | tf_op jit(solution)/shard_map/ppermute | solution.py:41
  1028.2 293.7 %collective-permute-start.3 = (bf16[16,2,64,128]{3,0,1,2:T(8,128)(2,1)}, bf16[16,2,64,128]{3,0,1,2:T(8,128)(2,1)}, u32[]{:S(2)}, u32[]{:S(2)}) collective-permute-start(bf16[16,2,64,128]{3,0,1,2:T(8,128)(2,1)} %get-tuple-element.334), channel_id=1, source_target_pairs={{0,1},{1,2},{2,3},{3,4},{4,5},{5,6},{6,7},{7,8},{8,9},{9,10},{10,1... | collective-permute-start | bytes 1572872 | tf_op jit(solution)/shard_map/ppermute | solution.py:41
  1132.2 2.7 copy-start.9
  1134.9 2.5 copy-start.15
  1320.5 2.8 copy-start.23
  (41 other events, 56.3 us)
Sparse Core Ops, SparseCore 0:
  55.8 269.2 all-reduce.13
  956.7 175.5 all-reduce.15
where the time goes:
time: 1450 us; the launch traced here: 1440 us
  blocking collectives  538 us (37%)
  waiting for transfers between devices  353 us (24%)
  local copies, waits for them, and re-layouts  289 us (20%)
  matrix products  154 us (11%)
  other arithmetic  53.4 us (4%)
  starting transfers between devices  37.3 us (3%)
  between operations  14.9 us (1%)
    pmax x1, blocking collectives, shards(): edge_top = lax.pmax(jnp.max(edge_scores, axis=2), 'seq')  249 us
    psum x1, waiting for transfers between devices, broadcast(): return lax.psum(block, axis)  206 us
    psum x1, blocking collectives, shards(): edge_dquery_sum, global_sum = lax.psum((edge_dquery, global_part), 'seq')  123 us
    psum x1, blocking collectives, shards(): gain_grad = lax.psum(gain_term, ('dp', 'seq'))  106 us
    psum x1, waiting for transfers between devices, shards(): lax.psum((jnp.sum(edge_expo, axis=2), jnp.einsum('hqt,htd->hqd', edge_exp...  99.2 us
    psum x1, blocking collectives, shards(): lax.psum((jnp.sum(edge_expo, axis=2), jnp.einsum('hqt,htd->hqd', edge_exp...  59.2 us
    while x160, local copies, waits for them, and re-layouts  46.8 us
    dot_general x24, matrix products, spread_terms(): jnp.einsum('hpbc,hpbd->hpcd', coef_blocks[:, :, :, NG + offset], rows_in,...  41.4 us
  transfers between devices with their start and end apart: 9, of which 5 were waited for; matrix products, arithmetic and copies ran while one was open for 7% of the time, Pallas kernels for 0%

commit v1 on v0

--- a/solution.py
+++ b/solution.py
@@ -336,7 +336,7 @@
     gain_term = jnp.sum(key_eff_grad * to_heads(keys[0]).astype(jnp.float32), axis=(1, 2)).reshape(
         HEADS * HD
     )
-    gain_grad = lax.psum(gain_term, ("dp", "seq"))
+    gain_grad = lax.psum(lax.psum(gain_term, "dp"), "seq")
     return (
         from_heads(attended_all),
         from_heads(dquery_all),

time: 1450 us -> 1390 us (0.959)
  the two profiles are of different devices: /device:TPU:1 before, /device:TPU:0 now
where the time goes in v1:
time: 1390 us; the launch traced here: 1370 us
  blocking collectives  496 us (36%)
  waiting for transfers between devices  332 us (24%)
  local copies, waits for them, and re-layouts  288 us (21%)
  matrix products  154 us (11%)
  other arithmetic  53.3 us (4%)
  starting transfers between devices  35.1 us (3%)
  between operations  14.9 us (1%)
    pmax x1, blocking collectives, shards(): edge_top = lax.pmax(jnp.max(edge_scores, axis=2), 'seq')  258 us
    psum x1, waiting for transfers between devices, broadcast(): return lax.psum(block, axis)  205 us
    psum x1, blocking collectives, shards(): edge_dquery_sum, global_sum = lax.psum((edge_dquery, global_part), 'seq')  153 us
    psum x1, waiting for transfers between devices, shards(): lax.psum((jnp.sum(edge_expo, axis=2), jnp.einsum('hqt,htd->hqd', edge_exp...  76.1 us
    psum x1, blocking collectives, shards(): lax.psum((jnp.sum(edge_expo, axis=2), jnp.einsum('hqt,htd->hqd', edge_exp...  72.5 us
    while x160, local copies, waits for them, and re-layouts  46.8 us
    dot_general x24, matrix products, spread_terms(): jnp.einsum('hpbc,hpbd->hpcd', coef_blocks[:, :, :, NG + offset], rows_in,...  41.3 us
    unnamed x62, local copies, waits for them, and re-layouts  34 us
  transfers between devices with their start and end apart: 9, of which 5 were waited for; matrix products, arithmetic and copies ran while one was open for 7% of the time, Pallas kernels for 0%

profile of v1, /device:TPU:0, one launch (start us, length us, event | category | flops | bytes accessed | tf_op | source)
XLA Modules:
  0.0 1374.5 jit_solution(5641926175510165412)
XLA Ops:
  11.2 9.7 all-to-all-start
  20.9 2.8 convert_bitcast_fusion
  27.6 3.0 all-to-all-done
  32.5 10.3 gather_fusion
  42.8 6.9 all-to-all-start.1
  56.2 4.4 collective-permute-start
  66.9 25.1 %collective-permute-done = bf16[2,64,2048]{2,1,0:T(8,128)(2,1)} collective-permute-done((bf16[2,64,2048]{2,1,0:T(8,128)(2,1)}, bf16[2,64,2048]{2,1,0:T(8,128)(2,1)}, u32[]{:S(2)}, u32[]{:S(2)}) %collective-permute-start) | collective-permute-done | bytes 524320 | tf_op jit(solution)/shard_map/ppermute | solution.py:29
  92.0 23.1 %collective-permute-done.1 = bf16[2,64,2048]{2,1,0:T(8,128)(2,1)} collective-permute-done((bf16[2,64,2048]{2,1,0:T(8,128)(2,1)}, bf16[2,64,2048]{2,1,0:T(8,128)(2,1)}, u32[]{:S(2)}, u32[]{:S(2)}) %collective-permute-start.1) | collective-permute-done | bytes 524320 | tf_op jit(solution)/shard_map/ppermute | solution.py:31
  119.6 204.8 %all-reduce.15.cloned.1.call-done = bf16[4,128,2048]{2,1,0:T(8,128)(2,1)} async-done(((bf16[4,128,2048]{2,1,0:T(8,128)(2,1)}), bf16[4,128,2048]{2,1,0:T(8,128)(2,1)}) %all-reduce.15.cloned.1.call-update) | async-done | bytes 2097168 | tf_op jit(solution)/shard_map/psum | solution.py:18
  328.4 11.8 gather_fusion.1
  340.1 8.1 fusion.134
  348.2 287.8 %while.24 = (s32[]{:T(128)}, bf16[4,4,4,64,128]{4,3,2,1,0:T(8,128)(2,1)}, bf16[4,4,4,64,128]{4,3,2,1,0:T(8,128)(2,1)}, f32[4,4,2,2,64,128]{5,1,0,2,4,3:T(4,128)}...) while((s32[]{:T(128)}, ...), condition=%wide.region_14.15_spmd.clone, body=%wide.region_10.14_spmd.clone.sunk | while | flops 952370176 | bytes 142396560 | solution.py:227
  355.7 3.5 fusion.232
  365.1 3.1 fusion.233
  368.2 5.2 bitcast_dynamic-update-slice_fusion.6
  374.5 3.2 multiply_convert_fusion.4
  385.0 2.9 fusion.240
  427.5 3.5 fusion.232
  436.9 3.1 fusion.233
  440.0 5.2 bitcast_dynamic-update-slice_fusion.6
  446.3 3.2 multiply_convert_fusion.4
  456.7 2.9 fusion.240
  499.2 3.5 fusion.232
  508.6 3.1 fusion.233
  511.7 5.2 bitcast_dynamic-update-slice_fusion.6
  518.0 3.2 multiply_convert_fusion.4
  528.5 2.9 fusion.240
  571.0 3.5 fusion.232
  580.4 3.1 fusion.233
  583.5 5.2 bitcast_dynamic-update-slice_fusion.6
  589.9 3.2 multiply_convert_fusion.4
  600.2 2.9 fusion.240
  636.0 12.7 copy.168
  648.7 10.8 reshape.529
  659.5 4.9 broadcast_in_dim.167
  664.4 28.8 %scatter_fusion = bf16[288,64,256]{2,1,0:T(8,128)(2,1)} fusion(bf16[288,64,256]{2,1,0:T(8,128)(2,1)} %broadcast_in_dim.167, s32[192]{0:T(256)S(1)} %bitcast.510, bf16[192,64,256]{2,1,0:T(8,128)(2,1)} %reshape.529), kind=kCustom, calls=%fused_computation.3 | custom fusion | bytes 18875136 | tf_op jit(solution)/shard_map/scatter | solution.py:294
  693.2 5.6 all-to-all-start.2
  702.7 257.8 %pmax.7 = f32[16,128]{1,0:T(8,128)S(1)} all-reduce(f32[16,128]{1,0:T(8,128)S(1)} %get-tuple-element.354), channel_id=1, replica_groups=mesh['dp'=8,'seq'=32] {'seq'}, use_global_device_ids=true, to_apply=%region_2.3 | all-reduce | flops 2048 | bytes 16384 | tf_op jit(solution)/shard_map/pmax | solution.py:251
  960.5 3.5 fusion.97
  967.8 72.5 %psum.51 = f32[16,128]{1,0:T(8,128)S(1)} all-reduce(f32[16,128]{1,0:T(8,128)S(1)} %fusion.95), channel_id=1, replica_groups=mesh['dp'=8,'seq'=32] {'seq'}, use_global_device_ids=true, to_apply=%region_5.6 | all-reduce | flops 2048 | bytes 16384 | tf_op jit(solution)/shard_map/psum | solution.py:253
  1040.4 2.9 fusion.104
  1049.1 5.5 collective-permute-start.3
  1054.6 76.1 %all-reduce.17.cloned.1.call-done = (f32[16,128,128]{2,1,0:T(8,128)}, f32[16,2,2,64,128]{4,0,1,3,2:T(8,128)}) async-done(((f32[16,128,128]{2,1,0:T(8,128)}, f32[16,2,2,64,128]{4,0,1,3,2:T(8,128)}), (f32[16,128,128]{2,1,0:T(8,128)}, f32[16,2,2,64,128]{4,0,1,3,2:T(8,128)})) %all-reduce.17.cloned.1.call-update) | async-done | bytes 3145744 | tf_op jit(solution)/shard_map/psum | solution.py:253
  1140.5 18.9 %copy.212 = bf16[36,8,64,256]{3,1,2,0:T(8,128)(2,1)} copy(bf16[36,8,64,256]{3,2,1,0:T(8,128)(2,1)} %bitcast.182) | data formatting | bytes 18874368
  1159.3 16.0 %dot_general.116 = bf16[64,2,128,288]{2,1,0,3:T(2,128)(2,1)} reshape(bf16[16384,288]{0,1:T(8,128)(2,1)} %bitcast.459) | data formatting | bytes 18874368 | tf_op jit(solution)/shard_map/dot_general | solution.py:302
  1175.3 12.3 fusion.85
  1193.8 12.6 psum.54
  1206.4 152.7 %all-reduce.18 = (bf16[16,2,64,128]{3,2,1,0:T(8,128)(2,1)S(1)}, f32[2048]{0:T(1024)}) all-reduce(f32[16,2,64,128]{3,2,1,0:T(8,128)S(1)} %bitcast.484, f32[2048]{0:T(1024)S(1)} %psum.54), channel_id=1, replica_groups=mesh['dp'=8,'seq'=32] {'seq'}, use_global_device_ids=true, to_apply=%region_16.17 | all-reduce | flops 264192 | bytes 1589248 | tf_op jit(solution)/shard_map/psum | solution.py:312
  (457 shorter events, 282.7 us)
Async XLA Ops:
  9.3 57.4 %copy-start.33 = (s32[192,1]{0,1:T(1,128)}, s32[192,1]{0,1:T(1,128)S(1)}, u32[]{:S(2)}) copy-start(s32[192,1]{0,1:T(1,128)S(1)} %compare_select_fusion.1) | copy-start | bytes 2308
  11.2 19.4 %all-to-all-start = ((s32[32,1,9]{2,1,0:T(1,128)}), s32[32,1,9]{2,1,0:T(1,128)S(1)}, u32[]{:S(2)}, u32[]{:S(2)}) async-start(s32[32,1,9]{2,1,0:T(1,128)} %bitcast.20), calls=%async_computation | async-start | bytes 32768 | tf_op jit(solution)/shard_map/all_to_all | solution.py:182
  42.8 285.6 %all-to-all-start.1 = ((bf16[32,9,64,256]{3,2,1,0:T(8,128)(2,1)}), bf16[32,9,64,256]{3,2,1,0:T(8,128)(2,1)}, u32[]{:S(2)}, u32[]{:S(2)}) async-start(bf16[32,9,64,256]{3,2,1,0:T(8,128)(2,1)} %bitcast.458), calls=%async_computation.1 | async-start | bytes 18874368 | tf_op jit(solution)/shard_map/all_to_all | solution.py:185
  49.7 274.7 %all-reduce.15.cloned.1.call-start = ((), (), s32[]{:S(2)}) async-start(), calls=%async_computation.3 | async-start | bytes 4194304 | tf_op jit(solution)/shard_map/psum | solution.py:18
  56.2 35.7 %collective-permute-start = (bf16[2,64,2048]{2,1,0:T(8,128)(2,1)}, bf16[2,64,2048]{2,1,0:T(8,128)(2,1)}, u32[]{:S(2)}, u32[]{:S(2)}) collective-permute-start(bf16[2,64,2048]{2,1,0:T(8,128)(2,1)} %get-tuple-element.344), channel_id=1, source_target_pairs={{0,1},{1,2},{2,3},{3,4},{4,5},{5,6},{6,7},{7,8},{8,9},{9,10},{10,1... | collective-permute-start | bytes 1572872 | tf_op jit(solution)/shard_map/ppermute | solution.py:29
  60.6 54.4 %collective-permute-start.1 = (bf16[2,64,2048]{2,1,0:T(8,128)(2,1)}, bf16[2,64,2048]{2,1,0:T(8,128)(2,1)}, u32[]{:S(2)}, u32[]{:S(2)}) collective-permute-start(bf16[2,64,2048]{2,1,0:T(8,128)(2,1)} %get-tuple-element.345), channel_id=1, source_target_pairs={{1,0},{2,1},{3,2},{4,3},{5,4},{6,5},{7,6},{8,7},{9,8},{10,9},{11,1... | collective-permute-start | bytes 1572872 | tf_op jit(solution)/shard_map/ppermute | solution.py:31
  62.4 2.8 copy-start.24
  355.5 3.7 copy-start.1
  362.2 2.9 copy-start.2
  379.8 3.8 copy-start.5
  382.1 2.9 copy-start
  409.5 2.6 copy-start.4
  416.1 2.7 copy-start.3
  416.2 2.7 copy-start.28
  427.3 3.7 copy-start.1
  434.0 2.9 copy-start.2
  451.6 3.8 copy-start.5
  453.8 2.9 copy-start
  481.2 2.6 copy-start.4
  487.9 2.7 copy-start.3
  487.9 2.6 copy-start.28
  499.0 3.7 copy-start.1
  505.7 2.9 copy-start.2
  523.3 3.8 copy-start.5
  525.6 3.0 copy-start
  553.0 2.6 copy-start.4
  559.7 2.7 copy-start.3
  559.7 2.7 copy-start.28
  570.8 3.7 copy-start.1
  577.5 2.9 copy-start.2
  595.1 3.8 copy-start.5
  597.4 2.9 copy-start
  624.7 2.6 copy-start.4
  631.5 2.7 copy-start.3
  631.5 2.7 copy-start.28
  659.5 4.9 copy-start.34
  693.2 5.7 copy-start.7
  693.2 5.7 copy-start.31
  693.2 447.3 %all-to-all-start.2 = ((bf16[32,9,64,256]{3,2,1,0:T(8,128)(2,1)}), bf16[32,9,64,256]{3,2,1,0:T(8,128)(2,1)}, u32[]{:S(2)}, u32[]{:S(2)}) async-start(bf16[32,9,64,256]{3,2,1,0:T(8,128)(2,1)} %bitcast.456), calls=%async_computation.2 | async-start | bytes 18874368 | tf_op jit(solution)/shard_map/all_to_all | solution.py:297
  698.8 432.0 %all-reduce.17.cloned.1.call-start = ((), (), s32[]{:S(2)}) async-start(), calls=%async_computation.4 | async-start | bytes 6291456 | tf_op jit(solution)/shard_map/psum | solution.py:253
  1040.4 5.5 slice-start.1
  1040.4 5.5 slice-start.2
  1047.8 139.8 %collective-permute-start.2 = (bf16[16,2,64,128]{3,0,1,2:T(8,128)(2,1)}, bf16[16,2,64,128]{3,0,1,2:T(8,128)(2,1)}, u32[]{:S(2)}, u32[]{:S(2)}) collective-permute-start(bf16[16,2,64,128]{3,0,1,2:T(8,128)(2,1)} %get-tuple-element.337), channel_id=1, source_target_pairs={{1,0},{2,1},{3,2},{4,3},{5,4},{6,5},{7,6},{8,7},{9,8},{10,9},{11,1... | collective-permute-start | bytes 1572872 | tf_op jit(solution)/shard_map/ppermute | solution.py:41
  1049.1 140.0 %collective-permute-start.3 = (bf16[16,2,64,128]{3,0,1,2:T(8,128)(2,1)}, bf16[16,2,64,128]{3,0,1,2:T(8,128)(2,1)}, u32[]{:S(2)}, u32[]{:S(2)}) collective-permute-start(bf16[16,2,64,128]{3,0,1,2:T(8,128)(2,1)} %get-tuple-element.336), channel_id=1, source_target_pairs={{0,1},{1,2},{2,3},{3,4},{4,5},{5,6},{6,7},{7,8},{8,9},{9,10},{10,1... | collective-permute-start | bytes 1572872 | tf_op jit(solution)/shard_map/ppermute | solution.py:41
  1130.8 2.7 copy-start.9
  1187.6 2.8 copy-start.25
  1192.4 14.1 %copy-start.18 = (f32[16,128,128]{2,1,0:T(8,128)S(1)}, f32[16,128,128]{2,1,0:T(8,128)}, u32[]{:S(2)}) copy-start(f32[16,128,128]{2,1,0:T(8,128)} %fusion.110) | copy-start | bytes 3145732
  1363.7 2.5 copy-start.20
  (43 other events, 61.7 us)
Sparse Core Ops, SparseCore 0:
  54.1 270.2 all-reduce.14
  964.2 166.5 all-reduce.16
